TPU v7x, 32 devices: a whole 2x2x4 slice. The times are simulated.
32 devices in a mesh: ens: 2 (over core), gy: 4 (over y, x), gz: 4 (over z).
Axes of the slice: x: 2, y: 2, z: 4, core: 2. Of those that a mesh axis runs over, the one named last changes fastest.
Arguments:
- state: float32 [2, 4, 16, 64, 512], P('ens', None, None, 'gy', 'gz'), parts along dimension 0, may hold values from -32 to 32
- member_set: int32 [2], P('ens'), parts along dimension 0, may hold values from 0 to 15
- courant_table: float32 [16, 3], replicated, may hold values from -0.3 to 0.3
- diffusion_table: float32 [16, 4], replicated, may hold values from 0.05 to 1
- reaction_table: float32 [16, 4, 4], replicated, may hold values from -3 to 3
- quadratic_table: float32 [16, 4], replicated, may hold values from -1 to 1
Outputs:
- state_out: float32 [2, 4, 16, 64, 512], P('ens', None, None, 'gy', 'gz'), parts along dimension 0
There are 2 independent parts, one for each index of `ens`. A program takes and returns all parts, laid end to end along the dimension named above; an argument that names none is the same for every part. Nothing has to cross between parts.
All inputs are finite; a program needn't handle non-finite values.
Results may differ from a plain program's by a relative error of at most 0.00024.
Values sent between devices are 32-bit elements; how exact they have to be, the bound alone decides.
A program may use at most 64 MiB of HBM per device.

v0:
```python
import jax
import jax.numpy as jnp
from jax import lax
from jax.sharding import PartitionSpec as P

ITERS = 4


def extended(cells, sides, width):
    for axis, dim in sides:
        count = lax.axis_size(axis)
        ends = count - 1
        head = lax.slice_in_dim(cells, 0, width, axis=dim)
        tail = lax.slice_in_dim(cells, cells.shape[dim] - width, cells.shape[dim], axis=dim)
        cells = jnp.concatenate(
            [
                lax.ppermute(tail, axis, [(i, (i + 1) % count) for i in range(ends)]),
                cells,
                lax.ppermute(head, axis, [((i + 1) % count, i) for i in range(ends)]),
            ],
            axis=dim,
        )
    return cells


def lookup(member_set, coeff_table):
    onehot = (
        member_set[:, None] == jnp.arange(coeff_table.shape[0], dtype=jnp.int32)[None, :]
    ).astype(coeff_table.dtype)
    flattened = coeff_table.reshape(coeff_table.shape[0], -1)
    picked = jnp.sum(onehot[:, :, None] * flattened[None, :, :], axis=1)
    return picked.reshape((member_set.shape[0],) + coeff_table.shape[1:])


def spread_out(values):
    return values[:, None, None, None, None]


def beside_all(padded, spatial, offset):
    slicer = [slice(None), slice(None), slice(1, -1), slice(1, -1), slice(1, -1)]
    slicer[spatial] = slice(offset, padded.shape[spatial] - 2 + offset)
    return padded[tuple(slicer)]


def explicit_section(padded, current, courant, reaction, quadratic):
    running = current
    for spatial in range(3):
        velocity = spread_out(courant[:, spatial])
        behind = beside_all(padded, spatial + 2, 0)
        beyond = beside_all(padded, spatial + 2, 2)
        running = (
            running
            - jnp.maximum(velocity, 0.0) * (current - behind)
            - jnp.minimum(velocity, 0.0) * (beyond - current)
        )
    linear = jnp.einsum("mkl,mlxyz->mkxyz", reaction, current, precision=lax.Precision.HIGHEST)
    leading = current[:, 0]
    partner = current[:, 1]
    coupled = leading * partner / (1.0 + leading * leading + partner * partner)
    return running + linear + quadratic[:, :, None, None, None] * coupled[:, None]


def implicit_apply(padded, current, diffuse):
    beside = beside_all(padded, 2, 0) + beside_all(padded, 2, 2)
    beside = beside + beside_all(padded, 3, 0) + beside_all(padded, 3, 2)
    beside = beside + beside_all(padded, 4, 0) + beside_all(padded, 4, 2)
    strength = diffuse[:, :, None, None, None]
    return (1.0 + 6.0 * strength) * current - strength * beside


def inner_product(left_side, right_side):
    return jnp.sum(left_side * right_side, axis=(1, 2, 3, 4))


def least_squares(hessen, beta, iters):
    target = [beta] + [jnp.zeros_like(beta)] * iters
    cosines = []
    sine_list = []
    triangle = []
    for column in range(iters):
        entries = list(hessen[column])
        for earlier in range(column):
            rotated = (
                cosines[earlier] * entries[earlier] + sine_list[earlier] * entries[earlier + 1]
            )
            entries[earlier + 1] = (
                -sine_list[earlier] * entries[earlier] + cosines[earlier] * entries[earlier + 1]
            )
            entries[earlier] = rotated
        radius = jnp.sqrt(
            entries[column] * entries[column] + entries[column + 1] * entries[column + 1]
        )
        cosine = entries[column] / radius
        sine_val = entries[column + 1] / radius
        entries[column] = radius
        target[column + 1] = -sine_val * target[column]
        target[column] = cosine * target[column]
        cosines.append(cosine)
        sine_list.append(sine_val)
        triangle.append(entries[: column + 1])
    coeffs = [None] * iters
    for column in reversed(range(iters)):
        running = target[column]
        for further in range(column + 1, iters):
            running = running - triangle[further][column] * coeffs[further]
        coeffs[column] = running / triangle[column][column]
    return coeffs


def pad_first_dim(padded):
    return jnp.pad(padded, ((0, 0), (0, 0), (1, 1), (0, 0), (0, 0)))


def exchange_rim(current):
    padded = extended(current, (("gy", 3), ("gz", 4)), 1)
    return pad_first_dim(padded)


def normalized(unscaled, factor):
    vector = unscaled * spread_out(factor)
    rimmed = exchange_rim(vector)
    return (vector, rimmed)


def shards(state, member_set, courant_table, diffusion_table, reaction_table, quadratic_table):
    courant = lookup(member_set, courant_table)
    diffuse = lookup(member_set, diffusion_table)
    reaction = lookup(member_set, reaction_table)
    quadratic = lookup(member_set, quadratic_table)
    padded = extended(state, (("gy", 3), ("gz", 4)), 1)
    source = explicit_section(pad_first_dim(padded), state, courant, reaction, quadratic)
    beta = jnp.sqrt(lax.psum(inner_product(source, source), ("gy", "gz")))
    vector, rimmed = normalized(source, 1.0 / beta)
    basis = [vector]
    hessen = []
    for column in range(ITERS):
        image = implicit_apply(rimmed, basis[column], diffuse)
        local_dots = jnp.stack(
            [inner_product(basis[earlier], image) for earlier in range(column + 1)], axis=1
        )
        projections, length_sq = lax.psum((local_dots, inner_product(image, image)), ("gy", "gz"))
        remainder = image
        for earlier in range(column + 1):
            remainder = remainder - spread_out(projections[:, earlier]) * basis[earlier]
        norm_next = jnp.sqrt(length_sq - jnp.sum(projections * projections, axis=1))
        hessen.append([projections[:, earlier] for earlier in range(column + 1)] + [norm_next])
        if column + 1 < ITERS:
            vector, rimmed = normalized(remainder, 1.0 / norm_next)
            basis.append(vector)
    coeffs = least_squares(hessen, beta, ITERS)
    state_out = spread_out(coeffs[0]) * basis[0]
    for column in range(1, ITERS):
        state_out = state_out + spread_out(coeffs[column]) * basis[column]
    return state_out


def solution(mesh):
    return jax.shard_map(
        shards,
        mesh=mesh,
        in_specs=(P("ens", None, None, "gy", "gz"), P("ens"), P(), P(), P(), P()),
        out_specs=P("ens", None, None, "gy", "gz"),
        check_vma=False,
    )
```

profile of v0, /device:TPU:0, one launch (start us, length us, event | category | flops | bytes accessed | tf_op | source)
XLA Modules:
  0.0 346.6 jit_solution(4202919764877653318)
XLA Ops:
  0.0 1.4 copy.73
  1.5 4.9 %collective-permute-start = (f32[1,4,16,1,128]{4,1,3,2,0:T(4,128)S(1)}, f32[1,4,16,1,128]{4,1,3,2,0:T(4,128)S(1)}, u32[]{:S(2)}, u32[]{:S(2)}) collective-permute-start(f32[1,4,16,1,128]{4,1,3,2,0:T(4,128)S(1)} %get-tuple-element.51), channel_id=1, source_target_pairs={{0,4},{4,8},{8,12},{1,5},{5,9},{9,13},{2,6},{6,10},{10,14},{3,7},{... | collective-permute-start | bytes 98312 | tf_op jit(solution)/shard_map/ppermute | solution.py:17
  6.4 1.3 collective-permute-start.1
  9.2 3.0 collective-permute-done.1
  13.0 3.5 %collective-permute-start.2 = (f32[1,4,16,18,1]{3,2,4,1,0:T(8,128)S(1)}, f32[1,4,16,18,1]{3,2,4,1,0:T(8,128)S(1)}, u32[]{:S(2)}, u32[]{:S(2)}) collective-permute-start(f32[1,4,16,18,1]{3,2,4,1,0:T(8,128)S(1)} %copy.68), channel_id=1, source_target_pairs={{0,1},{1,2},{2,3},{4,5},{5,6},{6,7},{8,9},{9,10},{10,11},{12,13},{... | collective-permute-start | bytes 13832 | tf_op jit(solution)/shard_map/ppermute | solution.py:17
  17.0 1.3 collective-permute-start.3
  23.8 1.0 select_maximum_fusion.16
  24.7 3.1 multiply_reduce_fusion.14
  27.9 42.1 %psum.63 = f32[1]{0:T(128)} all-reduce(f32[1]{0:T(128)} %bitcast.13), channel_id=1, replica_groups=mesh['ens'=2,'gy'=4,'gz'=4] {'gy','gz'}, use_global_device_ids=true, to_apply=%region_4.5 | all-reduce | flops 1 | bytes 8 | tf_op jit(solution)/shard_map/psum | solution.py:132
  70.8 1.3 collective-permute-start.4
  72.1 1.3 collective-permute-start.5
  73.7 7.5 %collective-permute-done.5 = f32[1,4,16,1,128]{4,1,3,2,0:T(4,128)S(1)} collective-permute-done((f32[1,4,16,1,128]{4,1,3,2,0:T(4,128)S(1)}, f32[1,4,16,1,128]{4,1,3,2,0:T(4,128)S(1)}, u32[]{:S(2)}, u32[]{:S(2)}) %collective-permute-start.5) | collective-permute-done | bytes 32800 | tf_op jit(solution)/shard_map/ppermute | solution.py:19
  82.2 1.3 collective-permute-start.6
  83.9 1.3 collective-permute-start.7
  85.8 4.0 %collective-permute-done.7 = f32[1,4,16,18,1]{3,2,4,1,0:T(8,128)S(1)} collective-permute-done((f32[1,4,16,18,1]{3,2,4,1,0:T(8,128)S(1)}, f32[1,4,16,18,1]{3,2,4,1,0:T(8,128)S(1)}, u32[]{:S(2)}, u32[]{:S(2)}) %collective-permute-start.7) | collective-permute-done | bytes 4640 | tf_op jit(solution)/shard_map/ppermute | solution.py:19
  90.3 1.0 select_maximum_fusion.12
  91.3 2.1 multiply_reduce_fusion.13
  93.4 37.5 %all-reduce.8 = (f32[1]{0:T(128)}, f32[1,1]{1,0:T(1,128)}) all-reduce(f32[1]{0:T(128)} %bitcast.17, f32[1,1]{1,0:T(1,128)} %bitcast.15), channel_id=1, replica_groups=mesh['ens'=2,'gy'=4,'gz'=4] {'gy','gz'}, use_global_device_ids=true, to_apply=%region_9.10 | all-reduce | flops 2 | bytes 16 | tf_op jit(solution)/shard_map/psum | solution.py:141
  133.7 1.3 collective-permute-start.8
  135.0 1.3 collective-permute-start.9
  136.5 5.8 %collective-permute-done.9 = f32[1,4,16,1,128]{4,1,3,2,0:T(4,128)S(1)} collective-permute-done((f32[1,4,16,1,128]{4,1,3,2,0:T(4,128)S(1)}, f32[1,4,16,1,128]{4,1,3,2,0:T(4,128)S(1)}, u32[]{:S(2)}, u32[]{:S(2)}) %collective-permute-start.9) | collective-permute-done | bytes 32800 | tf_op jit(solution)/shard_map/ppermute | solution.py:19
  143.3 3.5 collective-permute-start.10
  147.3 1.5 collective-permute-start.11
  149.3 3.8 %collective-permute-done.11 = f32[1,4,16,18,1]{3,2,4,1,0:T(8,128)S(1)} collective-permute-done((f32[1,4,16,18,1]{3,2,4,1,0:T(8,128)S(1)}, f32[1,4,16,18,1]{3,2,4,1,0:T(8,128)S(1)}, u32[]{:S(2)}, u32[]{:S(2)}) %collective-permute-start.11) | collective-permute-done | bytes 4640 | tf_op jit(solution)/shard_map/ppermute | solution.py:19
  153.6 1.0 select_maximum_fusion.8
  154.6 2.1 multiply_reduce_fusion.11
  156.7 1.3 pad_maximum_fusion.40
  158.0 37.4 %all-reduce.7 = (f32[1]{0:T(128)}, f32[1,2]{1,0:T(1,128)S(1)}) all-reduce(f32[1]{0:T(128)} %bitcast.25, f32[1,2]{1,0:T(1,128)S(1)} %pad_maximum_fusion.40), channel_id=1, replica_groups=mesh['ens'=2,'gy'=4,'gz'=4] {'gy','gz'}, use_global_device_ids=true, to_apply=%region_14.15 | all-reduce | flops 3 | bytes 24 | tf_op jit(solution)/shard_map/psum | solution.py:141
  198.0 1.3 subtract_multiply_fusion.1
  199.4 1.3 collective-permute-start.12
  200.7 1.3 collective-permute-start.13
  202.3 5.5 %collective-permute-done.13 = f32[1,4,16,1,128]{4,1,3,2,0:T(4,128)S(1)} collective-permute-done((f32[1,4,16,1,128]{4,1,3,2,0:T(4,128)S(1)}, f32[1,4,16,1,128]{4,1,3,2,0:T(4,128)S(1)}, u32[]{:S(2)}, u32[]{:S(2)}) %collective-permute-start.13) | collective-permute-done | bytes 32800 | tf_op jit(solution)/shard_map/ppermute | solution.py:19
  208.8 3.8 %collective-permute-start.14 = (f32[1,4,16,18,1]{3,2,4,1,0:T(8,128)S(1)}, f32[1,4,16,18,1]{3,2,4,1,0:T(8,128)S(1)}, u32[]{:S(2)}, u32[]{:S(2)}) collective-permute-start(f32[1,4,16,18,1]{3,2,4,1,0:T(8,128)S(1)} %copy.96), channel_id=1, source_target_pairs={{0,1},{1,2},{2,3},{4,5},{5,6},{6,7},{8,9},{9,10},{10,11},{12,13},{... | collective-permute-start | bytes 13832 | tf_op jit(solution)/shard_map/ppermute | solution.py:17
  213.1 1.3 collective-permute-start.15
  214.9 4.0 %collective-permute-done.15 = f32[1,4,16,18,1]{3,2,4,1,0:T(8,128)S(1)} collective-permute-done((f32[1,4,16,18,1]{3,2,4,1,0:T(8,128)S(1)}, f32[1,4,16,18,1]{3,2,4,1,0:T(8,128)S(1)}, u32[]{:S(2)}, u32[]{:S(2)}) %collective-permute-start.15) | collective-permute-done | bytes 4640 | tf_op jit(solution)/shard_map/ppermute | solution.py:19
  220.4 2.5 multiply_reduce_fusion.8
  222.9 1.9 pad_maximum_fusion.41
  224.8 37.4 %all-reduce.6 = (f32[1]{0:T(128)}, f32[1,3]{1,0:T(1,128)S(1)}) all-reduce(f32[1]{0:T(128)} %bitcast.36, f32[1,3]{1,0:T(1,128)S(1)} %pad_maximum_fusion.41), channel_id=1, replica_groups=mesh['ens'=2,'gy'=4,'gz'=4] {'gy','gz'}, use_global_device_ids=true, to_apply=%region_21.22 | all-reduce | flops 4 | bytes 32 | tf_op jit(solution)/shard_map/psum | solution.py:141
  264.7 2.1 subtract_multiply_fusion
  266.8 1.3 collective-permute-start.16
  268.1 1.3 collective-permute-start.17
  269.7 5.5 %collective-permute-done.17 = f32[1,4,16,1,128]{4,1,3,2,0:T(4,128)S(1)} collective-permute-done((f32[1,4,16,1,128]{4,1,3,2,0:T(4,128)S(1)}, f32[1,4,16,1,128]{4,1,3,2,0:T(4,128)S(1)}, u32[]{:S(2)}, u32[]{:S(2)}) %collective-permute-start.17) | collective-permute-done | bytes 32800 | tf_op jit(solution)/shard_map/ppermute | solution.py:19
  276.2 3.9 %collective-permute-start.18 = (f32[1,4,16,18,1]{3,2,4,1,0:T(8,128)S(1)}, f32[1,4,16,18,1]{3,2,4,1,0:T(8,128)S(1)}, u32[]{:S(2)}, u32[]{:S(2)}) collective-permute-start(f32[1,4,16,18,1]{3,2,4,1,0:T(8,128)S(1)} %copy.102), channel_id=1, source_target_pairs={{0,1},{1,2},{2,3},{4,5},{5,6},{6,7},{8,9},{9,10},{10,11},{12,13},{... | collective-permute-start | bytes 13832 | tf_op jit(solution)/shard_map/ppermute | solution.py:17
  280.6 1.3 collective-permute-start.19
  291.5 1.0 select_maximum_fusion
  292.5 2.6 multiply_reduce_fusion
  295.0 2.6 pad_maximum_fusion.42
  297.6 40.1 %all-reduce.5 = (f32[1,4]{1,0:T(1,128)S(1)}, f32[1]{0:T(128)}) all-reduce(f32[1,4]{1,0:T(1,128)S(1)} %pad_maximum_fusion.42, f32[1]{0:T(128)} %bitcast.50), channel_id=1, replica_groups=mesh['ens'=2,'gy'=4,'gz'=4] {'gy','gz'}, use_global_device_ids=true, to_apply=%region_27.28 | all-reduce | flops 5 | bytes 40 | tf_op jit(solution)/shard_map/psum | solution.py:141
  (78 shorter events, 21.6 us)
Async XLA Ops:
  0.0 7.7 %copy-start = (f32[1,4,16,16,128]{4,3,2,1,0:T(8,128)S(1)}, f32[1,4,16,16,128]{4,3,2,1,0:T(8,128)}, u32[]{:S(2)}) copy-start(f32[1,4,16,16,128]{4,3,2,1,0:T(8,128)} %param.6) | copy-start | bytes 1572868
  0.0 8.4 %copy-start.1 = (f32[16,4,4]{0,2,1:T(4,128)S(1)}, f32[16,4,4]{0,2,1:T(4,128)}, u32[]{:S(2)}) copy-start(f32[16,4,4]{0,2,1:T(4,128)} %param.10) | copy-start | bytes 3076
  0.0 8.5 %copy-start.4 = (f32[16,4]{0,1:T(4,128)S(1)}, f32[16,4]{0,1:T(4,128)}, u32[]{:S(2)}) copy-start(f32[16,4]{0,1:T(4,128)} %param.11) | copy-start | bytes 772
  0.0 8.5 %copy-start.3 = (f32[16,4]{0,1:T(4,128)S(1)}, f32[16,4]{0,1:T(4,128)}, u32[]{:S(2)}) copy-start(f32[16,4]{0,1:T(4,128)} %param.9) | copy-start | bytes 772
  0.0 8.7 %copy-start.2 = (f32[16,3]{0,1:T(4,128)S(1)}, f32[16,3]{0,1:T(4,128)}, u32[]{:S(2)}) copy-start(f32[16,3]{0,1:T(4,128)} %param.8) | copy-start | bytes 580
  1.5 7.3 %collective-permute-start = (f32[1,4,16,1,128]{4,1,3,2,0:T(4,128)S(1)}, f32[1,4,16,1,128]{4,1,3,2,0:T(4,128)S(1)}, u32[]{:S(2)}, u32[]{:S(2)}) collective-permute-start(f32[1,4,16,1,128]{4,1,3,2,0:T(4,128)S(1)} %get-tuple-element.51), channel_id=1, source_target_pairs={{0,4},{4,8},{8,12},{1,5},{5,9},{9,13},{2,6},{6,10},{10,14},{3,7},{... | collective-permute-start | bytes 98312 | tf_op jit(solution)/shard_map/ppermute | solution.py:17
  6.4 5.8 %collective-permute-start.1 = (f32[1,4,16,1,128]{4,1,3,2,0:T(4,128)S(1)}, f32[1,4,16,1,128]{4,1,3,2,0:T(4,128)S(1)}, u32[]{:S(2)}, u32[]{:S(2)}) collective-permute-start(f32[1,4,16,1,128]{4,1,3,2,0:T(4,128)S(1)} %get-tuple-element.50), channel_id=1, source_target_pairs={{4,0},{8,4},{12,8},{5,1},{9,5},{13,9},{6,2},{10,6},{14,10},{7,3},{... | collective-permute-start | bytes 98312 | tf_op jit(solution)/shard_map/ppermute | solution.py:19
  13.0 9.7 %collective-permute-start.2 = (f32[1,4,16,18,1]{3,2,4,1,0:T(8,128)S(1)}, f32[1,4,16,18,1]{3,2,4,1,0:T(8,128)S(1)}, u32[]{:S(2)}, u32[]{:S(2)}) collective-permute-start(f32[1,4,16,18,1]{3,2,4,1,0:T(8,128)S(1)} %copy.68), channel_id=1, source_target_pairs={{0,1},{1,2},{2,3},{4,5},{5,6},{6,7},{8,9},{9,10},{10,11},{12,13},{... | collective-permute-start | bytes 13832 | tf_op jit(solution)/shard_map/ppermute | solution.py:17
  17.0 6.2 %collective-permute-start.3 = (f32[1,4,16,18,1]{3,2,4,1,0:T(8,128)S(1)}, f32[1,4,16,18,1]{3,2,4,1,0:T(8,128)S(1)}, u32[]{:S(2)}, u32[]{:S(2)}) collective-permute-start(f32[1,4,16,18,1]{3,2,4,1,0:T(8,128)S(1)} %copy.69), channel_id=1, source_target_pairs={{1,0},{2,1},{3,2},{5,4},{6,5},{7,6},{9,8},{10,9},{11,10},{13,12},{... | collective-permute-start | bytes 13832 | tf_op jit(solution)/shard_map/ppermute | solution.py:19
  70.8 2.9 collective-permute-start.4
  72.1 9.1 %collective-permute-start.5 = (f32[1,4,16,1,128]{4,1,3,2,0:T(4,128)S(1)}, f32[1,4,16,1,128]{4,1,3,2,0:T(4,128)S(1)}, u32[]{:S(2)}, u32[]{:S(2)}) collective-permute-start(f32[1,4,16,1,128]{4,1,3,2,0:T(4,128)S(1)} %get-tuple-element.49), channel_id=1, source_target_pairs={{4,0},{8,4},{12,8},{5,1},{9,5},{13,9},{6,2},{10,6},{14,10},{7,3},{... | collective-permute-start | bytes 98312 | tf_op jit(solution)/shard_map/ppermute | solution.py:19
  82.2 3.1 collective-permute-start.6
  83.9 5.8 %collective-permute-start.7 = (f32[1,4,16,18,1]{3,2,4,1,0:T(8,128)S(1)}, f32[1,4,16,18,1]{3,2,4,1,0:T(8,128)S(1)}, u32[]{:S(2)}, u32[]{:S(2)}) collective-permute-start(f32[1,4,16,18,1]{3,2,4,1,0:T(8,128)S(1)} %copy.85), channel_id=1, source_target_pairs={{1,0},{2,1},{3,2},{5,4},{6,5},{7,6},{9,8},{10,9},{11,10},{13,12},{... | collective-permute-start | bytes 13832 | tf_op jit(solution)/shard_map/ppermute | solution.py:19
  133.7 2.9 collective-permute-start.8
  135.0 7.4 %collective-permute-start.9 = (f32[1,4,16,1,128]{4,1,3,2,0:T(4,128)S(1)}, f32[1,4,16,1,128]{4,1,3,2,0:T(4,128)S(1)}, u32[]{:S(2)}, u32[]{:S(2)}) collective-permute-start(f32[1,4,16,1,128]{4,1,3,2,0:T(4,128)S(1)} %get-tuple-element.47), channel_id=1, source_target_pairs={{4,0},{8,4},{12,8},{5,1},{9,5},{13,9},{6,2},{10,6},{14,10},{7,3},{... | collective-permute-start | bytes 98312 | tf_op jit(solution)/shard_map/ppermute | solution.py:19
  143.3 5.4 %collective-permute-start.10 = (f32[1,4,16,18,1]{3,2,4,1,0:T(8,128)S(1)}, f32[1,4,16,18,1]{3,2,4,1,0:T(8,128)S(1)}, u32[]{:S(2)}, u32[]{:S(2)}) collective-permute-start(f32[1,4,16,18,1]{3,2,4,1,0:T(8,128)S(1)} %copy.90), channel_id=1, source_target_pairs={{0,1},{1,2},{2,3},{4,5},{5,6},{6,7},{8,9},{9,10},{10,11},{12,13},{... | collective-permute-start | bytes 13832 | tf_op jit(solution)/shard_map/ppermute | solution.py:17
  147.3 5.8 %collective-permute-start.11 = (f32[1,4,16,18,1]{3,2,4,1,0:T(8,128)S(1)}, f32[1,4,16,18,1]{3,2,4,1,0:T(8,128)S(1)}, u32[]{:S(2)}, u32[]{:S(2)}) collective-permute-start(f32[1,4,16,18,1]{3,2,4,1,0:T(8,128)S(1)} %copy.91), channel_id=1, source_target_pairs={{1,0},{2,1},{3,2},{5,4},{6,5},{7,6},{9,8},{10,9},{11,10},{13,12},{... | collective-permute-start | bytes 13832 | tf_op jit(solution)/shard_map/ppermute | solution.py:19
  199.4 2.9 collective-permute-start.12
  200.7 7.1 %collective-permute-start.13 = (f32[1,4,16,1,128]{4,1,3,2,0:T(4,128)S(1)}, f32[1,4,16,1,128]{4,1,3,2,0:T(4,128)S(1)}, u32[]{:S(2)}, u32[]{:S(2)}) collective-permute-start(f32[1,4,16,1,128]{4,1,3,2,0:T(4,128)S(1)} %get-tuple-element.45), channel_id=1, source_target_pairs={{4,0},{8,4},{12,8},{5,1},{9,5},{13,9},{6,2},{10,6},{14,10},{7,3},{... | collective-permute-start | bytes 98312 | tf_op jit(solution)/shard_map/ppermute | solution.py:19
  208.8 5.6 %collective-permute-start.14 = (f32[1,4,16,18,1]{3,2,4,1,0:T(8,128)S(1)}, f32[1,4,16,18,1]{3,2,4,1,0:T(8,128)S(1)}, u32[]{:S(2)}, u32[]{:S(2)}) collective-permute-start(f32[1,4,16,18,1]{3,2,4,1,0:T(8,128)S(1)} %copy.96), channel_id=1, source_target_pairs={{0,1},{1,2},{2,3},{4,5},{5,6},{6,7},{8,9},{9,10},{10,11},{12,13},{... | collective-permute-start | bytes 13832 | tf_op jit(solution)/shard_map/ppermute | solution.py:17
  213.1 5.8 %collective-permute-start.15 = (f32[1,4,16,18,1]{3,2,4,1,0:T(8,128)S(1)}, f32[1,4,16,18,1]{3,2,4,1,0:T(8,128)S(1)}, u32[]{:S(2)}, u32[]{:S(2)}) collective-permute-start(f32[1,4,16,18,1]{3,2,4,1,0:T(8,128)S(1)} %copy.97), channel_id=1, source_target_pairs={{1,0},{2,1},{3,2},{5,4},{6,5},{7,6},{9,8},{10,9},{11,10},{13,12},{... | collective-permute-start | bytes 13832 | tf_op jit(solution)/shard_map/ppermute | solution.py:19
  266.8 2.9 collective-permute-start.16
  268.1 7.1 %collective-permute-start.17 = (f32[1,4,16,1,128]{4,1,3,2,0:T(4,128)S(1)}, f32[1,4,16,1,128]{4,1,3,2,0:T(4,128)S(1)}, u32[]{:S(2)}, u32[]{:S(2)}) collective-permute-start(f32[1,4,16,1,128]{4,1,3,2,0:T(4,128)S(1)} %get-tuple-element.43), channel_id=1, source_target_pairs={{4,0},{8,4},{12,8},{5,1},{9,5},{13,9},{6,2},{10,6},{14,10},{7,3},{... | collective-permute-start | bytes 98312 | tf_op jit(solution)/shard_map/ppermute | solution.py:19
  276.2 14.2 %collective-permute-start.18 = (f32[1,4,16,18,1]{3,2,4,1,0:T(8,128)S(1)}, f32[1,4,16,18,1]{3,2,4,1,0:T(8,128)S(1)}, u32[]{:S(2)}, u32[]{:S(2)}) collective-permute-start(f32[1,4,16,18,1]{3,2,4,1,0:T(8,128)S(1)} %copy.102), channel_id=1, source_target_pairs={{0,1},{1,2},{2,3},{4,5},{5,6},{6,7},{8,9},{9,10},{10,11},{12,13},{... | collective-permute-start | bytes 13832 | tf_op jit(solution)/shard_map/ppermute | solution.py:17
  280.6 10.4 %collective-permute-start.19 = (f32[1,4,16,18,1]{3,2,4,1,0:T(8,128)S(1)}, f32[1,4,16,18,1]{3,2,4,1,0:T(8,128)S(1)}, u32[]{:S(2)}, u32[]{:S(2)}) collective-permute-start(f32[1,4,16,18,1]{3,2,4,1,0:T(8,128)S(1)} %copy.103), channel_id=1, source_target_pairs={{1,0},{2,1},{3,2},{5,4},{6,5},{7,6},{9,8},{10,9},{11,10},{13,12},{... | collective-permute-start | bytes 13832 | tf_op jit(solution)/shard_map/ppermute | solution.py:19
where the time goes:
time: 348 us; the launch traced here: 347 us
  blocking collectives  194 us (56%)
  waiting for transfers between devices  40.3 us (12%)
  starting transfers between devices  39 us (11%)
  other arithmetic  27.4 us (8%)
  between operations  25.3 us (7%)
  local copies, waits for them, and re-layouts  17 us (5%)
    psum x4, blocking collectives, shards(): lax.psum((local_dots, inner_product(image, image)), ('gy', 'gz'))  152 us
    psum x1, blocking collectives, shards(): beta = jnp.sqrt(lax.psum(inner_product(source, source), ('gy', 'gz')))  42.1 us
    ppermute x10, waiting for transfers between devices, extended(): lax.ppermute(head, axis, [((i + 1) % count, i) for i in range(ends)])  39.1 us
    ppermute x10, starting transfers between devices, extended(): lax.ppermute(tail, axis, [(i, (i + 1) % count) for i in range(ends)])  26 us
    ppermute x10, starting transfers between devices, extended(): lax.ppermute(head, axis, [((i + 1) % count, i) for i in range(ends)])  13.1 us
    reduce_sum x4, other arithmetic, inner_product(): return jnp.sum(left_side * right_side, axis=(1, 2, 3, 4))  9.34 us
  transfers between devices with their start and end apart: 20, of which 12 were waited for; matrix products, arithmetic and copies ran while one was open for 2% of the time, Pallas kernels for 0%

commit v1 on v0

v1 whole, which is shorter than its diff:
```python
import functools

import jax
import jax.numpy as jnp
from jax import lax
from jax.experimental import pallas as pl
from jax.experimental.pallas import tpu as pltpu
from jax.sharding import PartitionSpec as P

ITERS = 4
TOP = 8


def kernel(
    ny, nz,
    state_ref, set_ref, courant_ref, diffuse_ref, react_ref, quad_ref,
    out_ref,
    cells, padded, image, basis,
    ysend, yrecv, zsend, zrecv, dsend, drecv,
    ysend_sem, yrecv_sem, zsend_sem, zrecv_sem, dsend_sem, drecv_sem, load_sem,
):
    species, xs, ys, lanes = cells.shape
    count = ny * nz
    gy, gz = lax.axis_index("gy"), lax.axis_index("gz")
    me = gy * nz + gz
    low, high = TOP - 1, TOP + ys
    halo_rounds = ITERS + 1

    load = pltpu.make_async_copy(state_ref.at[0], cells, load_sem)
    load.start()

    def peer(step):
        other = lax.rem(me + step, count)
        return {"gy": lax.div(other, nz), "gz": lax.rem(other, nz)}

    barrier = pltpu.get_barrier_semaphore()
    for step in range(1, count):
        pl.semaphore_signal(
            barrier, inc=1, device_id=peer(step), device_id_type=pl.DeviceIdType.MESH
        )

    slab = jnp.zeros((ys, lanes), jnp.float32)
    for k in range(species):
        for edge in (0, xs + 1):
            where = k * (xs + 2) + edge
            padded[where, TOP:high, :] = slab
            for j in range(ITERS):
                basis[j, where, TOP:high, :] = slab
    for side, outermost in ((0, gy == 0), (1, gy == ny - 1)):
        @pl.when(outermost)
        def _():
            for r in range(halo_rounds):
                yrecv[r, side] = jnp.zeros(yrecv.shape[2:], jnp.float32)
    for side, outermost in ((0, gz == 0), (1, gz == nz - 1)):
        @pl.when(outermost)
        def _():
            for r in range(halo_rounds):
                zrecv[r, side] = jnp.zeros(zrecv.shape[2:], jnp.float32)

    lane = lax.broadcasted_iota(jnp.int32, (ys, lanes), 1)
    odd = lax.rem(lane, 2) == 1
    first, last = lane == 0, lane == lanes - 1

    def halo_copies(r):
        listed = []
        for side, there, inside in ((0, 1, gy > 0), (1, 0, gy < ny - 1)):
            listed.append((inside, gy < ny - 1 if side == 0 else gy > 0,
                pltpu.make_async_remote_copy(
                    src_ref=ysend.at[r, side], dst_ref=yrecv.at[r, there],
                    send_sem=ysend_sem.at[r, side], recv_sem=yrecv_sem.at[r, there],
                    device_id={"gy": gy - 1 if side == 0 else gy + 1},
                    device_id_type=pl.DeviceIdType.MESH)))
        for side, there, inside in ((0, 1, gz > 0), (1, 0, gz < nz - 1)):
            listed.append((inside, gz < nz - 1 if side == 0 else gz > 0,
                pltpu.make_async_remote_copy(
                    src_ref=zsend.at[r], dst_ref=zrecv.at[r, there],
                    send_sem=zsend_sem.at[r, side], recv_sem=zrecv_sem.at[r, there],
                    device_id={"gz": gz - 1 if side == 0 else gz + 1},
                    device_id_type=pl.DeviceIdType.MESH)))
        return listed

    def start_halo(r):
        for inside, _, copy in halo_copies(r):
            @pl.when(inside)
            def _():
                copy.start()

    def finish_halo(r):
        for _, arriving, copy in halo_copies(r):
            @pl.when(arriving)
            def _():
                copy.wait_recv()
        return jnp.where(odd, zrecv[r, 0], pltpu.roll(zrecv[r, 1], lanes - 2, 1))

    def slot(k, x):
        return k * (xs + 2) + x + 1, k * xs + x

    def pack(zpack, block, r, k, x):
        _, j = slot(k, x)
        ysend[r, 0, pl.ds(j, 1), :] = block[0:1, :]
        ysend[r, 1, pl.ds(j, 1), :] = block[ys - 1 : ys, :]
        turned = pltpu.roll(block, 2 * j, 1)
        here = (lane == 2 * j) | (lane == lax.rem(2 * j + lanes - 1, lanes))
        return jnp.where(here, turned, zpack)

    def beside(ref, lead, zhalo, k, x):
        i, j = slot(k, x)
        at = lambda a, b: ref[lead + (a, slice(b, b + ys), slice(None))]
        here = at(i, TOP)
        edge = pltpu.roll(zhalo, lax.rem(lanes + 1 - 2 * j + lanes, lanes), 1)
        before = jnp.where(first, edge, pltpu.roll(here, 1, 1))
        after = jnp.where(last, edge, pltpu.roll(here, lanes - 1, 1))
        return (here, (at(i - 1, TOP), at(i + 1, TOP)), (at(i, TOP - 1), at(i, TOP + 1)),
                (before, after))

    def fold(value):
        total = value[0:8]
        for row in range(8, ys, 8):
            total = total + value[row : row + 8]
        return total

    load.wait()

    def take(x, zpack):
        for k in range(species):
            block = cells[k, x]
            padded[slot(k, x)[0], TOP:high, :] = block
            zpack = pack(zpack, block, 0, k, x)
        return zpack

    zsend[0] = lax.fori_loop(0, xs, take, jnp.zeros((ys, lanes), jnp.float32))
    pl.semaphore_wait(barrier, count - 1)
    start_halo(0)

    member = set_ref[0]
    courant = [courant_ref[member, d] for d in range(3)]
    strength = [diffuse_ref[member, k] for k in range(species)]
    rates = [[react_ref[member, k, l] for l in range(species)] for k in range(species)]
    coupling = [quad_ref[member, k] for k in range(species)]
    ahead = [jnp.maximum(c, 0.0) for c in courant]
    back = [jnp.minimum(c, 0.0) for c in courant]
    keep = 1.0
    for d in range(3):
        keep = keep - ahead[d] + back[d]

    zhalo = finish_halo(0)

    def set_rows(ref, lead, r, k, x):
        i, j = slot(k, x)
        ref[lead + (i, slice(low, low + 1), slice(None))] = yrecv[r, 0, pl.ds(j, 1), :]
        ref[lead + (i, slice(high, high + 1), slice(None))] = yrecv[r, 1, pl.ds(j, 1), :]

    def explicit(x, zpack):
        near = []
        for k in range(species):
            set_rows(padded, (), 0, k, x)
        for k in range(species):
            near.append(beside(padded, (), zhalo, k, x))
        a, b = near[0][0], near[1][0]
        coupled = a * b / (1.0 + a * a + b * b)
        for k in range(species):
            here = near[k][0]
            total = keep * here
            for d in range(3):
                total = total + ahead[d] * near[k][1 + d][0] - back[d] * near[k][1 + d][1]
            for l in range(species):
                total = total + rates[k][l] * near[l][0]
            total = total + coupling[k] * coupled
            basis[0, slot(k, x)[0], TOP:high, :] = total
            zpack = pack(zpack, total, 1, k, x)
        return zpack

    zsend[1] = lax.fori_loop(0, xs, explicit, jnp.zeros((ys, lanes), jnp.float32))
    start_halo(1)
    halos = [finish_halo(1)]

    def rows0(x, carry):
        for k in range(species):
            set_rows(basis, (0,), 1, k, x)
        return carry

    lax.fori_loop(0, xs, rows0, 0)

    def total_of(grid, row):
        return jnp.sum(grid[row : row + 1, :], axis=1, keepdims=True)

    cosines, sines, triangle = [], [], []
    target = None

    def rotate(entries, column):
        for earlier in range(column):
            rotated = cosines[earlier] * entries[earlier] + sines[earlier] * entries[earlier + 1]
            entries[earlier + 1] = (
                cosines[earlier] * entries[earlier + 1] - sines[earlier] * entries[earlier]
            )
            entries[earlier] = rotated
        radius = jnp.sqrt(
            entries[column] * entries[column] + entries[column + 1] * entries[column + 1]
        )
        cosine, sine = entries[column] / radius, entries[column + 1] / radius
        cosines.append(cosine)
        sines.append(sine)
        triangle.append(entries[:column] + [radius])
        target.append(-sine * target[column])
        target[column] = cosine * target[column]

    pending = None
    inverse_beta = None
    for column in range(ITERS):
        more = column + 1 < ITERS
        r = column + 2
        zhalo = halos[column]
        products = column + 1 + (2 if column == 0 else 1)

        def implicit(x, carry):
            zpack, sums = carry[0], list(carry[1:])
            for k in range(species):
                here, nearx, neary, nearz = beside(basis, (column,), zhalo, k, x)
                around = nearx[0] + nearx[1] + (neary[0] + neary[1]) + (nearz[0] + nearz[1])
                made = (1.0 + 6.0 * strength[k]) * here - strength[k] * around
                i = slot(k, x)[0]
                image[i, TOP:high, :] = made
                if more:
                    zpack = pack(zpack, made, r, k, x)
                for earlier in range(column):
                    sums[earlier] = sums[earlier] + fold(basis[earlier, i, TOP:high, :] * made)
                sums[column] = sums[column] + fold(here * made)
                sums[column + 1] = sums[column + 1] + fold(made * made)
                if column == 0:
                    sums[2] = sums[2] + fold(here * here)
            return (zpack, *sums)

        zero = jnp.zeros((8, lanes), jnp.float32)
        result = lax.fori_loop(
            0, xs, implicit, (jnp.zeros((ys, lanes), jnp.float32),) + (zero,) * products
        )
        rows = [jnp.sum(part, axis=0, keepdims=True) for part in result[1:]]
        mine = jnp.zeros((8, lanes), jnp.float32)
        row_of = lax.broadcasted_iota(jnp.int32, (8, lanes), 0)
        for p in range(products):
            mine = jnp.where(row_of == p, rows[p], mine)
        dsend[column] = mine
        for step in range(1, count):
            pltpu.make_async_remote_copy(
                src_ref=dsend.at[column], dst_ref=drecv.at[column, me],
                send_sem=dsend_sem.at[column], recv_sem=drecv_sem.at[column],
                device_id=peer(step), device_id_type=pl.DeviceIdType.MESH,
            ).start()
        if more:
            zsend[r] = result[0]
            start_halo(r)
        drecv[column, me] = mine
        if pending is not None:
            rotate(*pending)
        others = drecv.at[column, pl.ds(0, count - 1)]
        pltpu.make_async_copy(others, others, drecv_sem.at[column]).wait()
        grid = drecv[column, 0]
        for other in range(1, count):
            grid = grid + drecv[column, other]
        sums = [total_of(grid, p) for p in range(products)]
        if column == 0:
            beta = jnp.sqrt(sums[2])
            inverse_beta = 1.0 / beta
            target = [beta]
            square = inverse_beta * inverse_beta
            projections = [sums[0] * square]
            length_sq = sums[1] * square
        else:
            projections = [sums[0] * inverse_beta] + sums[1 : column + 1]
            length_sq = sums[column + 1]
        kept = projections[0] * projections[0]
        for value in projections[1:]:
            kept = kept + value * value
        norm_next = jnp.sqrt(length_sq - kept)
        pending = (projections + [norm_next], column)
        if not more:
            break
        inverse = 1.0 / norm_next
        gain = inverse if column else inverse * inverse_beta
        gains = [-(projections[0] * inverse) * inverse_beta] + [
            -(value * inverse) for value in projections[1:]
        ]
        zhalo_new = finish_halo(r) * gain
        for earlier in range(column + 1):
            zhalo_new = zhalo_new + halos[earlier] * gains[earlier]
        halos.append(zhalo_new)
        wide = jnp.broadcast_to(gain, (ys, lanes))
        wides = [jnp.broadcast_to(g, (ys, lanes)) for g in gains]

        def combine(x, carry):
            for k in range(species):
                i, j = slot(k, x)
                total = image[i, TOP:high, :] * wide
                below = yrecv[r, 0, pl.ds(j, 1), :] * wide[0:1]
                above = yrecv[r, 1, pl.ds(j, 1), :] * wide[0:1]
                for earlier in range(column + 1):
                    total = total + basis[earlier, i, TOP:high, :] * wides[earlier]
                    below = below + basis[earlier, i, low : low + 1, :] * wides[earlier][0:1]
                    above = above + basis[earlier, i, high : high + 1, :] * wides[earlier][0:1]
                basis[column + 1, i, TOP:high, :] = total
                basis[column + 1, i, low : low + 1, :] = below
                basis[column + 1, i, high : high + 1, :] = above
            return carry

        lax.fori_loop(0, xs, combine, 0)

    rotate(*pending)
    coeffs = [None] * ITERS
    for column in reversed(range(ITERS)):
        running = target[column]
        for further in range(column + 1, ITERS):
            running = running - triangle[further][column] * coeffs[further]
        coeffs[column] = running / triangle[column][column]
    coeffs[0] = coeffs[0] * inverse_beta
    wides = [jnp.broadcast_to(c, (ys, lanes)) for c in coeffs]

    def finish(x, carry):
        for k in range(species):
            i = slot(k, x)[0]
            total = basis[0, i, TOP:high, :] * wides[0]
            for column in range(1, ITERS):
                total = total + basis[column, i, TOP:high, :] * wides[column]
            out_ref[0, k, x] = total
        return carry

    lax.fori_loop(0, xs, finish, 0)

    for r in range(halo_rounds):
        for inside, _, copy in halo_copies(r):
            @pl.when(inside)
            def _():
                copy.wait_send()
    for column in range(ITERS):
        others = drecv.at[column, pl.ds(0, count - 1)]
        pltpu.make_async_copy(others, others, dsend_sem.at[column]).wait()


def shards(ny, nz, state, member_set, courant, diffusion, reaction, quadratic):
    _, species, xs, ys, lanes = state.shape
    blocks, tall = species * (xs + 2), TOP + ys + 8
    rounds, count = ITERS + 1, ny * nz
    f32 = jnp.float32
    smem = pl.BlockSpec(memory_space=pltpu.SMEM)
    return pl.pallas_call(
        functools.partial(kernel, ny, nz),
        out_shape=jax.ShapeDtypeStruct(state.shape, f32),
        in_specs=[pl.BlockSpec(memory_space=pl.ANY)] + [smem] * 5,
        out_specs=pl.BlockSpec(memory_space=pltpu.VMEM),
        scratch_shapes=[
            pltpu.VMEM((species, xs, ys, lanes), f32),
            pltpu.VMEM((blocks, tall, lanes), f32),
            pltpu.VMEM((blocks, tall, lanes), f32),
            pltpu.VMEM((ITERS, blocks, tall, lanes), f32),
            pltpu.VMEM((rounds, 2, species * xs, lanes), f32),
            pltpu.VMEM((rounds, 2, species * xs, lanes), f32),
            pltpu.VMEM((rounds, ys, lanes), f32),
            pltpu.VMEM((rounds, 2, ys, lanes), f32),
            pltpu.VMEM((ITERS, 8, lanes), f32),
            pltpu.VMEM((ITERS, count, 8, lanes), f32),
            pltpu.SemaphoreType.DMA((rounds, 2)),
            pltpu.SemaphoreType.DMA((rounds, 2)),
            pltpu.SemaphoreType.DMA((rounds, 2)),
            pltpu.SemaphoreType.DMA((rounds, 2)),
            pltpu.SemaphoreType.DMA((ITERS,)),
            pltpu.SemaphoreType.DMA((ITERS,)),
            pltpu.SemaphoreType.DMA,
        ],
        compiler_params=pltpu.CompilerParams(collective_id=0, has_side_effects=True),
    )(state, member_set, courant, diffusion, reaction, quadratic)


def solution(mesh):
    return jax.shard_map(
        functools.partial(shards, mesh.shape["gy"], mesh.shape["gz"]),
        mesh=mesh,
        in_specs=(P("ens", None, None, "gy", "gz"), P("ens"), P(), P(), P(), P()),
        out_specs=P("ens", None, None, "gy", "gz"),
        check_vma=False,
    )
```

time: 348 us -> 58.7 us (0.17)
  blocking collectives: 194 us -> 0 us
  Pallas kernels: 0 us -> 52.3 us
  waiting for transfers between devices: 40.3 us -> 0 us
  starting transfers between devices: 39 us -> 0 us
  other arithmetic: 27.4 us -> 0 us
  between operations: 25.3 us -> 0.67 us
  local copies, waits for them, and re-layouts: 17 us -> 5.3 us
    psum x5 -> x0, blocking collectives: 194 us -> none  [the longest x4 152 us: shards(): lax.psum((local_dots, inner_product(image, image)), ('gy', 'gz'))]
    pallas_call x0 -> x1, Pallas kernels: none -> 52.3 us  [shards(): pl.pallas_call(functools.partial(kernel, ny, nz), out_shape=jax.ShapeDtyp...]
    ppermute x20 -> x0, waiting for transfers between devices: 40.3 us -> none  [the longest x10 39.1 us: extended(): lax.ppermute(head, axis, [((i + 1) % count, i) for i in range(ends)])]
    ppermute x20 -> x0, starting transfers between devices: 39 us -> none  [the longest x10 26 us: extended(): lax.ppermute(tail, axis, [(i, (i + 1) % count) for i in range(ends)])]
    reduce_sum x10 -> x0, other arithmetic: 11.6 us -> none  [the longest x4 9.34 us: inner_product(): return jnp.sum(left_side * right_side, axis=(1, 2, 3, 4))]
    slice x24 -> x0, local copies, waits for them, and re-layouts: 9.24 us -> none  [the longest x14 4.33 us: extended(): lax.slice_in_dim(cells, cells.shape[dim] - width, cells.shape[dim], axis=...]
    another operation x3 -> x0, other arithmetic: 5.82 us -> none  [shards(): jnp.stack([inner_product(basis[earlier], image) for earlier in range(colu...]
    concatenate x9 -> x0, other arithmetic: 5.45 us -> none  [extended(): jnp.concatenate([lax.ppermute(tail, axis, [(i, (i + 1) % count) for i in...]
  transfers between devices with their start and end apart: 20 -> 0, of which waited for: 12 -> 0; matrix products, arithmetic and copies ran while one was open for 2% -> 0% of each run, Pallas kernels for 0% -> 0%
where the time goes in v1:
time: 58.7 us; the launch traced here: 58.3 us
  Pallas kernels  52.3 us (89%)
  local copies, waits for them, and re-layouts  5.3 us (9%)
  between operations  0.67 us (1%)
    pallas_call x1, Pallas kernels, shards(): pl.pallas_call(functools.partial(kernel, ny, nz), out_shape=jax.ShapeDtyp...  52.3 us
    unnamed x11, local copies, waits for them, and re-layouts  5.3 us

profile of v1, /device:TPU:0, one launch (start us, length us, event | category | flops | bytes accessed | tf_op | source)
XLA Modules:
  0.0 58.3 jit_solution(631111464574744265)
XLA Ops:
  0.7 0.0 copy-start.1
  0.7 1.4 %copy.7.courant_ref = f32[16,3]{1,0:T(8,128)} copy(f32[16,3]{0,1:T(4,128)} %param.8) | data formatting | bytes 384 | tf_op args[2]
  2.0 0.0 copy-done.1
  2.0 0.0 copy-start.2
  2.0 0.0 copy-start
  2.0 0.7 %copy.8.diffuse_ref = f32[16,4]{1,0:T(8,128)} copy(f32[16,4]{0,1:T(4,128)S(1)} %copy-done.1) | data formatting | bytes 512 | tf_op args[3]
  2.7 0.0 copy-done.2
  2.7 0.7 %copy.10.quad_ref = f32[16,4]{1,0:T(8,128)} copy(f32[16,4]{0,1:T(4,128)S(1)} %copy-done.2) | data formatting | bytes 512 | tf_op args[5]
  3.4 0.0 copy-done
  3.4 0.7 %copy.9.react_ref = f32[16,4,4]{2,1,0:T(4,128)} copy(f32[16,4,4]{0,2,1:T(4,128)S(1)} %copy-done) | data formatting | bytes 2048 | tf_op args[4]
  4.1 52.3 %shard_map.64 = f32[1,4,16,16,128]{4,3,2,1,0:T(8,128)} custom-call(f32[1,4,16,16,128]{4,3,2,1,0:T(8,128)} %state_ref.1, s32[1]{0:T(128)S(6)} %copy.12.set_ref, f32[16,3]{1,0:T(8,128)} %copy.7.courant_ref, f32[16,4]{1,0:T(8,128)} %copy.8.diffuse_ref, f32[16,4,4]{2,1,0:T(4,128)} %copy.9.react_ref, f32[16,4]{1,0:T(8,128)} %copy.10.quad_ref), custom_call_target="tpu_custom_call" | custom-call | tf_op jit(solution)/shard_map/pallas_call | solution.py:344
  56.4 1.9 %copy.13 = f32[1,4,16,16,128]{4,3,2,1,0:T(8,128)} copy(f32[1,4,16,16,128]{4,3,2,1,0:T(8,128)} %shard_map.64) | data formatting | bytes 1048576
Async XLA Ops:
  0.7 1.4 %copy-start.1 = (f32[16,4]{0,1:T(4,128)S(1)}, f32[16,4]{0,1:T(4,128)}, u32[]{:S(2)}) copy-start(f32[16,4]{0,1:T(4,128)} %param.9) | copy-start | bytes 772
  2.0 0.7 %copy-start.2 = (f32[16,4]{0,1:T(4,128)S(1)}, f32[16,4]{0,1:T(4,128)}, u32[]{:S(2)}) copy-start(f32[16,4]{0,1:T(4,128)} %param.11) | copy-start | bytes 772
  2.0 1.4 %copy-start = (f32[16,4,4]{0,2,1:T(4,128)S(1)}, f32[16,4,4]{0,2,1:T(4,128)}, u32[]{:S(2)}) copy-start(f32[16,4,4]{0,2,1:T(4,128)} %param.10) | copy-start | bytes 3076

commit v2 on v1

--- a/solution.py
+++ b/solution.py
@@ -13,8 +13,9 @@
 
 def kernel(
     ny, nz,
-    state_ref, set_ref, courant_ref, diffuse_ref, react_ref, quad_ref,
+    state_ref, set_ref, courant_hbm, diffuse_hbm, react_hbm, quad_hbm,
     out_ref,
+    courant_ref, diffuse_ref, react_ref, quad_ref, table_sem,
     cells, padded, image, basis,
     ysend, yrecv, zsend, zrecv, dsend, drecv,
     ysend_sem, yrecv_sem, zsend_sem, zrecv_sem, dsend_sem, drecv_sem, load_sem,
@@ -28,6 +29,13 @@
 
     load = pltpu.make_async_copy(state_ref.at[0], cells, load_sem)
     load.start()
+    tables = [
+        pltpu.make_async_copy(source, target, table_sem.at[n])
+        for n, (source, target) in enumerate((
+            (courant_hbm, courant_ref), (diffuse_hbm, diffuse_ref), (react_hbm, react_ref), (quad_hbm, quad_ref)))
+    ]
+    for table in tables:
+        table.start()
 
     def peer(step):
         other = lax.rem(me + step, count)
@@ -128,15 +136,17 @@
             zpack = pack(zpack, block, 0, k, x)
         return zpack
 
-    zsend[0] = lax.fori_loop(0, xs, take, jnp.zeros((ys, lanes), jnp.float32))
+    zsend[0] = lax.fori_loop(0, xs, take, jnp.zeros((ys, lanes), jnp.float32), unroll=2)
     pl.semaphore_wait(barrier, count - 1)
     start_halo(0)
 
+    for table in tables:
+        table.wait()
     member = set_ref[0]
-    courant = [courant_ref[member, d] for d in range(3)]
-    strength = [diffuse_ref[member, k] for k in range(species)]
-    rates = [[react_ref[member, k, l] for l in range(species)] for k in range(species)]
-    coupling = [quad_ref[member, k] for k in range(species)]
+    courant = [courant_ref[d, member] for d in range(3)]
+    strength = [diffuse_ref[k, member] for k in range(species)]
+    rates = [[react_ref[k, l, member] for l in range(species)] for k in range(species)]
+    coupling = [quad_ref[k, member] for k in range(species)]
     ahead = [jnp.maximum(c, 0.0) for c in courant]
     back = [jnp.minimum(c, 0.0) for c in courant]
     keep = 1.0
@@ -170,7 +180,7 @@
             zpack = pack(zpack, total, 1, k, x)
         return zpack
 
-    zsend[1] = lax.fori_loop(0, xs, explicit, jnp.zeros((ys, lanes), jnp.float32))
+    zsend[1] = lax.fori_loop(0, xs, explicit, jnp.zeros((ys, lanes), jnp.float32), unroll=2)
     start_halo(1)
     halos = [finish_halo(1)]
 
@@ -179,10 +189,7 @@
             set_rows(basis, (0,), 1, k, x)
         return carry
 
-    lax.fori_loop(0, xs, rows0, 0)
-
-    def total_of(grid, row):
-        return jnp.sum(grid[row : row + 1, :], axis=1, keepdims=True)
+    lax.fori_loop(0, xs, rows0, 0, unroll=4)
 
     cosines, sines, triangle = [], [], []
     target = None
@@ -232,13 +239,13 @@
 
         zero = jnp.zeros((8, lanes), jnp.float32)
         result = lax.fori_loop(
-            0, xs, implicit, (jnp.zeros((ys, lanes), jnp.float32),) + (zero,) * products
+            0, xs, implicit, (jnp.zeros((ys, lanes), jnp.float32),) + (zero,) * products,
+            unroll=2,
         )
         rows = [jnp.sum(part, axis=0, keepdims=True) for part in result[1:]]
-        mine = jnp.zeros((8, lanes), jnp.float32)
-        row_of = lax.broadcasted_iota(jnp.int32, (8, lanes), 0)
+        mine = jnp.zeros((1, lanes), jnp.float32)
         for p in range(products):
-            mine = jnp.where(row_of == p, rows[p], mine)
+            mine = jnp.where(lane[0:1] == p, jnp.sum(rows[p], axis=1, keepdims=True), mine)
         dsend[column] = mine
         for step in range(1, count):
             pltpu.make_async_remote_copy(
@@ -257,7 +264,7 @@
         grid = drecv[column, 0]
         for other in range(1, count):
             grid = grid + drecv[column, other]
-        sums = [total_of(grid, p) for p in range(products)]
+        sums = [grid[:, p : p + 1] for p in range(products)]
         if column == 0:
             beta = jnp.sqrt(sums[2])
             inverse_beta = 1.0 / beta
@@ -302,7 +309,7 @@
                 basis[column + 1, i, high : high + 1, :] = above
             return carry
 
-        lax.fori_loop(0, xs, combine, 0)
+        lax.fori_loop(0, xs, combine, 0, unroll=2)
 
     rotate(*pending)
     coeffs = [None] * ITERS
@@ -323,7 +330,7 @@
             out_ref[0, k, x] = total
         return carry
 
-    lax.fori_loop(0, xs, finish, 0)
+    lax.fori_loop(0, xs, finish, 0, unroll=2)
 
     for r in range(halo_rounds):
         for inside, _, copy in halo_copies(r):
@@ -340,13 +347,15 @@
     blocks, tall = species * (xs + 2), TOP + ys + 8
     rounds, count = ITERS + 1, ny * nz
     f32 = jnp.float32
-    smem = pl.BlockSpec(memory_space=pltpu.SMEM)
+    anywhere = pl.BlockSpec(memory_space=pl.ANY)
+    tables = (courant.T, diffusion.T, jnp.transpose(reaction, (1, 2, 0)), quadratic.T)
     return pl.pallas_call(
         functools.partial(kernel, ny, nz),
-        out_shape=jax.ShapeDtypeStruct(state.shape, f32),
-        in_specs=[pl.BlockSpec(memory_space=pl.ANY)] + [smem] * 5,
+        out_shape=pltpu.VMEM(state.shape, f32),
+        in_specs=[anywhere, pl.BlockSpec(memory_space=pltpu.SMEM)] + [anywhere] * len(tables),
         out_specs=pl.BlockSpec(memory_space=pltpu.VMEM),
-        scratch_shapes=[
+        scratch_shapes=[pltpu.SMEM(table.shape, table.dtype) for table in tables] + [
+            pltpu.SemaphoreType.DMA((len(tables),)),
             pltpu.VMEM((species, xs, ys, lanes), f32),
             pltpu.VMEM((blocks, tall, lanes), f32),
             pltpu.VMEM((blocks, tall, lanes), f32),
@@ -355,8 +364,8 @@
             pltpu.VMEM((rounds, 2, species * xs, lanes), f32),
             pltpu.VMEM((rounds, ys, lanes), f32),
             pltpu.VMEM((rounds, 2, ys, lanes), f32),
-            pltpu.VMEM((ITERS, 8, lanes), f32),
-            pltpu.VMEM((ITERS, count, 8, lanes), f32),
+            pltpu.VMEM((ITERS, 1, lanes), f32),
+            pltpu.VMEM((ITERS, count, 1, lanes), f32),
             pltpu.SemaphoreType.DMA((rounds, 2)),
             pltpu.SemaphoreType.DMA((rounds, 2)),
             pltpu.SemaphoreType.DMA((rounds, 2)),
@@ -366,7 +375,7 @@
             pltpu.SemaphoreType.DMA,
         ],
         compiler_params=pltpu.CompilerParams(collective_id=0, has_side_effects=True),
-    )(state, member_set, courant, diffusion, reaction, quadratic)
+    )(state, member_set, *tables)
 
 
 def solution(mesh):

time: 58.7 us -> 44.5 us (0.76)
  Pallas kernels: 52.3 us -> 42.9 us
  local copies, waits for them, and re-layouts: 5.3 us -> 0.8 us
    pallas_call x1, Pallas kernels: 52.3 us -> 42.9 us  [shards(): pl.pallas_call(functools.partial(kernel, ny, nz), out_shape=pltpu.VMEM(st...]
    unnamed x11 -> x1, local copies, waits for them, and re-layouts: 5.3 us -> 0.8 us
where the time goes in v2:
time: 44.5 us; the launch traced here: 44.3 us
  Pallas kernels  42.9 us (96%)
  local copies, waits for them, and re-layouts  0.8 us (2%)
  between operations  0.66 us (1%)
    pallas_call x1, Pallas kernels, shards(): pl.pallas_call(functools.partial(kernel, ny, nz), out_shape=pltpu.VMEM(st...  42.9 us

profile of v2, /device:TPU:0, one launch (start us, length us, event | category | flops | bytes accessed | tf_op | source)
XLA Modules:
  0.0 44.3 jit_solution(16627046026896093864)
XLA Ops:
  0.7 42.9 %shard_map.64 = f32[1,4,16,16,128]{4,3,2,1,0:T(8,128)S(1)} custom-call(f32[1,4,16,16,128]{4,3,2,1,0:T(8,128)} %state_ref.1, s32[1]{0:T(128)S(6)} %copy.9.set_ref, f32[3,16]{1,0:T(4,128)} %bitcast.5, f32[4,16]{1,0:T(4,128)} %bitcast.6, f32[4,4,16]{2,1,0:T(4,128)} %bitcast.4, f32[4,16]{1,0:T(4,128)} %bitcast.7), custom_call_target="tpu_custom_call" | custom-call | tf_op jit(solution)/shard_map/pallas_call | solution.py:352
  43.5 0.8 %copy.8 = f32[1,4,16,16,128]{4,3,2,1,0:T(8,128)} copy(f32[1,4,16,16,128]{4,3,2,1,0:T(8,128)S(1)} %shard_map.64) | data formatting | bytes 1048576

commit v3 on v2

--- a/solution.py
+++ b/solution.py
@@ -16,7 +16,7 @@
     state_ref, set_ref, courant_hbm, diffuse_hbm, react_hbm, quad_hbm,
     out_ref,
     courant_ref, diffuse_ref, react_ref, quad_ref, table_sem,
-    cells, padded, image, basis,
+    cells, padded, further, images, basis,
     ysend, yrecv, zsend, zrecv, dsend, drecv,
     ysend_sem, yrecv_sem, zsend_sem, zrecv_sem, dsend_sem, drecv_sem, load_sem,
 ):
@@ -52,8 +52,9 @@
         for edge in (0, xs + 1):
             where = k * (xs + 2) + edge
             padded[where, TOP:high, :] = slab
-            for j in range(ITERS):
-                basis[j, where, TOP:high, :] = slab
+            for j in range(ITERS - 1):
+                images[j, where, TOP:high, :] = slab
+            basis[0, where, TOP:high, :] = slab
     for side, outermost in ((0, gy == 0), (1, gy == ny - 1)):
         @pl.when(outermost)
         def _():
@@ -182,7 +183,7 @@
 
     zsend[1] = lax.fori_loop(0, xs, explicit, jnp.zeros((ys, lanes), jnp.float32), unroll=2)
     start_halo(1)
-    halos = [finish_halo(1)]
+    zhalo = finish_halo(1)
 
     def rows0(x, carry):
         for k in range(species):
@@ -211,41 +212,19 @@
         target.append(-sine * target[column])
         target[column] = cosine * target[column]
 
-    pending = None
-    inverse_beta = None
-    for column in range(ITERS):
-        more = column + 1 < ITERS
-        r = column + 2
-        zhalo = halos[column]
-        products = column + 1 + (2 if column == 0 else 1)
-
-        def implicit(x, carry):
-            zpack, sums = carry[0], list(carry[1:])
-            for k in range(species):
-                here, nearx, neary, nearz = beside(basis, (column,), zhalo, k, x)
-                around = nearx[0] + nearx[1] + (neary[0] + neary[1]) + (nearz[0] + nearz[1])
-                made = (1.0 + 6.0 * strength[k]) * here - strength[k] * around
-                i = slot(k, x)[0]
-                image[i, TOP:high, :] = made
-                if more:
-                    zpack = pack(zpack, made, r, k, x)
-                for earlier in range(column):
-                    sums[earlier] = sums[earlier] + fold(basis[earlier, i, TOP:high, :] * made)
-                sums[column] = sums[column] + fold(here * made)
-                sums[column + 1] = sums[column + 1] + fold(made * made)
-                if column == 0:
-                    sums[2] = sums[2] + fold(here * here)
-            return (zpack, *sums)
-
-        zero = jnp.zeros((8, lanes), jnp.float32)
-        result = lax.fori_loop(
-            0, xs, implicit, (jnp.zeros((ys, lanes), jnp.float32),) + (zero,) * products,
-            unroll=2,
-        )
-        rows = [jnp.sum(part, axis=0, keepdims=True) for part in result[1:]]
+    zero = jnp.zeros((8, lanes), jnp.float32)
+    blank = jnp.zeros((ys, lanes), jnp.float32)
+
+    def applied(ref, lead, k, x, halo):
+        here, nearx, neary, nearz = beside(ref, lead, halo, k, x)
+        around = nearx[0] + nearx[1] + (neary[0] + neary[1]) + (nearz[0] + nearz[1])
+        return here, (1.0 + 6.0 * strength[k]) * here - strength[k] * around
+
+    def share(column, parts):
         mine = jnp.zeros((1, lanes), jnp.float32)
-        for p in range(products):
-            mine = jnp.where(lane[0:1] == p, jnp.sum(rows[p], axis=1, keepdims=True), mine)
+        for p, part in enumerate(parts):
+            row = jnp.sum(part, axis=0, keepdims=True)
+            mine = jnp.where(lane[0:1] == p, jnp.sum(row, axis=1, keepdims=True), mine)
         dsend[column] = mine
         for step in range(1, count):
             pltpu.make_async_remote_copy(
@@ -253,18 +232,61 @@
                 send_sem=dsend_sem.at[column], recv_sem=drecv_sem.at[column],
                 device_id=peer(step), device_id_type=pl.DeviceIdType.MESH,
             ).start()
-        if more:
-            zsend[r] = result[0]
-            start_halo(r)
         drecv[column, me] = mine
-        if pending is not None:
-            rotate(*pending)
+
+    def gathered(column, products):
         others = drecv.at[column, pl.ds(0, count - 1)]
         pltpu.make_async_copy(others, others, drecv_sem.at[column]).wait()
         grid = drecv[column, 0]
         for other in range(1, count):
             grid = grid + drecv[column, other]
-        sums = [grid[:, p : p + 1] for p in range(products)]
+        return [grid[:, p : p + 1] for p in range(products)]
+
+    def implicit(x, carry):
+        zpack, cross, square, own = carry
+        for k in range(species):
+            here, made = applied(basis, (0,), k, x, zhalo)
+            images[0, slot(k, x)[0], TOP:high, :] = made
+            zpack = pack(zpack, made, 2, k, x)
+            cross = cross + fold(here * made)
+            square = square + fold(made * made)
+            own = own + fold(here * here)
+        return zpack, cross, square, own
+
+    zpack, *parts = lax.fori_loop(0, xs, implicit, (blank, zero, zero, zero), unroll=2)
+    share(0, parts)
+    zsend[2] = zpack
+    start_halo(2)
+    halos = [finish_halo(2)]
+
+    def rows1(x, carry):
+        for k in range(species):
+            set_rows(images, (0,), 2, k, x)
+        return carry
+
+    lax.fori_loop(0, xs, rows1, 0, unroll=4)
+
+    pending = None
+    for column in range(ITERS):
+        more = column + 1 < ITERS
+        wider = column + 2 < ITERS
+        r = column + 3
+        if more:
+            def again(x, zpack):
+                for k in range(species):
+                    _, made = applied(images, (column,), k, x, halos[column])
+                    further[slot(k, x)[0]] = made
+                    if wider:
+                        zpack = pack(zpack, made, r, k, x)
+                return zpack
+
+            zpack = lax.fori_loop(0, xs, again, blank, unroll=2)
+            if wider:
+                zsend[r] = zpack
+                start_halo(r)
+        if pending is not None:
+            rotate(*pending)
+        sums = gathered(column, 3 if column == 0 else column + 2)
         if column == 0:
             beta = jnp.sqrt(sums[2])
             inverse_beta = 1.0 / beta
@@ -287,29 +309,43 @@
         gains = [-(projections[0] * inverse) * inverse_beta] + [
             -(value * inverse) for value in projections[1:]
         ]
-        zhalo_new = finish_halo(r) * gain
-        for earlier in range(column + 1):
-            zhalo_new = zhalo_new + halos[earlier] * gains[earlier]
-        halos.append(zhalo_new)
         wide = jnp.broadcast_to(gain, (ys, lanes))
         wides = [jnp.broadcast_to(g, (ys, lanes)) for g in gains]
 
-        def combine(x, carry):
+        def combine(x, sums):
+            sums = list(sums)
             for k in range(species):
-                i, j = slot(k, x)
-                total = image[i, TOP:high, :] * wide
-                below = yrecv[r, 0, pl.ds(j, 1), :] * wide[0:1]
-                above = yrecv[r, 1, pl.ds(j, 1), :] * wide[0:1]
+                i = slot(k, x)[0]
+                olds = [basis[earlier, i, TOP:high, :] for earlier in range(column + 1)]
+                vector = images[column, i, TOP:high, :] * wide
+                made = further[i] * wide
                 for earlier in range(column + 1):
-                    total = total + basis[earlier, i, TOP:high, :] * wides[earlier]
-                    below = below + basis[earlier, i, low : low + 1, :] * wides[earlier][0:1]
-                    above = above + basis[earlier, i, high : high + 1, :] * wides[earlier][0:1]
-                basis[column + 1, i, TOP:high, :] = total
-                basis[column + 1, i, low : low + 1, :] = below
-                basis[column + 1, i, high : high + 1, :] = above
-            return carry
-
-        lax.fori_loop(0, xs, combine, 0, unroll=2)
+                    vector = vector + olds[earlier] * wides[earlier]
+                    made = made + images[earlier, i, TOP:high, :] * wides[earlier]
+                basis[column + 1, i, TOP:high, :] = vector
+                images[column + 1, i, TOP:high, :] = made
+                for p, left in enumerate(olds + [vector, made]):
+                    sums[p] = sums[p] + fold(left * made)
+            return tuple(sums)
+
+        share(column + 1, lax.fori_loop(0, xs, combine, (zero,) * (column + 3), unroll=2))
+        if wider:
+            fresh = finish_halo(r) * gain
+            for earlier in range(column + 1):
+                fresh = fresh + halos[earlier] * gains[earlier]
+            halos.append(fresh)
+
+            def borders(x, carry):
+                for k in range(species):
+                    i, j = slot(k, x)
+                    for side, row in ((0, low), (1, high)):
+                        line = yrecv[r, side, pl.ds(j, 1), :] * wide[0:1]
+                        for earlier in range(column + 1):
+                            line = line + images[earlier, i, row : row + 1, :] * wides[earlier][0:1]
+                        images[column + 1, i, row : row + 1, :] = line
+                return carry
+
+            lax.fori_loop(0, xs, borders, 0, unroll=2)
 
     rotate(*pending)
     coeffs = [None] * ITERS
@@ -358,7 +394,8 @@
             pltpu.SemaphoreType.DMA((len(tables),)),
             pltpu.VMEM((species, xs, ys, lanes), f32),
             pltpu.VMEM((blocks, tall, lanes), f32),
-            pltpu.VMEM((blocks, tall, lanes), f32),
+            pltpu.VMEM((blocks, ys, lanes), f32),
+            pltpu.VMEM((ITERS, blocks, tall, lanes), f32),
             pltpu.VMEM((ITERS, blocks, tall, lanes), f32),
             pltpu.VMEM((rounds, 2, species * xs, lanes), f32),
             pltpu.VMEM((rounds, 2, species * xs, lanes), f32),

time: 44.5 us -> 41 us (0.921)
  Pallas kernels: 42.9 us -> 39.4 us
    pallas_call x1, Pallas kernels: 42.9 us -> 39.4 us  [shards(): pl.pallas_call(functools.partial(kernel, ny, nz), out_shape=pltpu.VMEM(st...]
where the time goes in v3:
time: 41 us; the launch traced here: 40.9 us
  Pallas kernels  39.4 us (96%)
  local copies, waits for them, and re-layouts  0.8 us (2%)
  between operations  0.66 us (2%)
    pallas_call x1, Pallas kernels, shards(): pl.pallas_call(functools.partial(kernel, ny, nz), out_shape=pltpu.VMEM(st...  39.4 us

profile of v3, /device:TPU:0, one launch (start us, length us, event | category | flops | bytes accessed | tf_op | source)
XLA Modules:
  0.0 40.9 jit_solution(14550146259482848850)
XLA Ops:
  0.7 39.4 %shard_map.64 = f32[1,4,16,16,128]{4,3,2,1,0:T(8,128)S(1)} custom-call(f32[1,4,16,16,128]{4,3,2,1,0:T(8,128)} %state_ref.1, s32[1]{0:T(128)S(6)} %copy.9.set_ref, f32[3,16]{1,0:T(4,128)} %bitcast.5, f32[4,16]{1,0:T(4,128)} %bitcast.6, f32[4,4,16]{2,1,0:T(4,128)} %bitcast.4, f32[4,16]{1,0:T(4,128)} %bitcast.7), custom_call_target="tpu_custom_call" | custom-call | tf_op jit(solution)/shard_map/pallas_call | solution.py:388
  40.1 0.8 %copy.8 = f32[1,4,16,16,128]{4,3,2,1,0:T(8,128)} copy(f32[1,4,16,16,128]{4,3,2,1,0:T(8,128)S(1)} %shard_map.64) | data formatting | bytes 1048576

commit v4 on v3

--- a/solution.py
+++ b/solution.py
@@ -69,6 +69,9 @@
     lane = lax.broadcasted_iota(jnp.int32, (ys, lanes), 1)
     odd = lax.rem(lane, 2) == 1
     first, last = lane == 0, lane == lanes - 1
+    line_of = lax.broadcasted_iota(jnp.int32, (ys, lanes), 0)
+    top, bottom = line_of == 0, line_of == ys - 1
+    empty = jnp.zeros((1, lanes), jnp.float32)
 
     def halo_copies(r):
         listed = []
@@ -112,11 +115,22 @@
         here = (lane == 2 * j) | (lane == lax.rem(2 * j + lanes - 1, lanes))
         return jnp.where(here, turned, zpack)
 
+    def turned_back(zhalo, j):
+        return pltpu.roll(zhalo, lax.rem(lanes + 1 - 2 * j + lanes, lanes), 1)
+
+    def outer(r, zhalo, k, x, below, above, before, after):
+        _, j = slot(k, x)
+        edge = turned_back(zhalo, j)
+        lines = jnp.where(
+            top, yrecv[r, 0, pl.ds(j, 1), :] * below,
+            jnp.where(bottom, yrecv[r, 1, pl.ds(j, 1), :] * above, 0.0))
+        return lines + jnp.where(first, edge * before, jnp.where(last, edge * after, 0.0))
+
     def beside(ref, lead, zhalo, k, x):
         i, j = slot(k, x)
         at = lambda a, b: ref[lead + (a, slice(b, b + ys), slice(None))]
         here = at(i, TOP)
-        edge = pltpu.roll(zhalo, lax.rem(lanes + 1 - 2 * j + lanes, lanes), 1)
+        edge = 0.0 if zhalo is None else turned_back(zhalo, j)
         before = jnp.where(first, edge, pltpu.roll(here, 1, 1))
         after = jnp.where(last, edge, pltpu.roll(here, lanes - 1, 1))
         return (here, (at(i - 1, TOP), at(i + 1, TOP)), (at(i, TOP - 1), at(i, TOP + 1)),
@@ -133,7 +147,10 @@
     def take(x, zpack):
         for k in range(species):
             block = cells[k, x]
-            padded[slot(k, x)[0], TOP:high, :] = block
+            i = slot(k, x)[0]
+            padded[i, TOP:high, :] = block
+            padded[i, low : low + 1, :] = empty
+            padded[i, high : high + 1, :] = empty
             zpack = pack(zpack, block, 0, k, x)
         return zpack
 
@@ -154,19 +171,13 @@
     for d in range(3):
         keep = keep - ahead[d] + back[d]
 
-    zhalo = finish_halo(0)
-
     def set_rows(ref, lead, r, k, x):
         i, j = slot(k, x)
         ref[lead + (i, slice(low, low + 1), slice(None))] = yrecv[r, 0, pl.ds(j, 1), :]
         ref[lead + (i, slice(high, high + 1), slice(None))] = yrecv[r, 1, pl.ds(j, 1), :]
 
-    def explicit(x, zpack):
-        near = []
-        for k in range(species):
-            set_rows(padded, (), 0, k, x)
-        for k in range(species):
-            near.append(beside(padded, (), zhalo, k, x))
+    def explicit(x, carry):
+        near = [beside(padded, (), None, k, x) for k in range(species)]
         a, b = near[0][0], near[1][0]
         coupled = a * b / (1.0 + a * a + b * b)
         for k in range(species):
@@ -176,21 +187,27 @@
                 total = total + ahead[d] * near[k][1 + d][0] - back[d] * near[k][1 + d][1]
             for l in range(species):
                 total = total + rates[k][l] * near[l][0]
-            total = total + coupling[k] * coupled
-            basis[0, slot(k, x)[0], TOP:high, :] = total
+            i = slot(k, x)[0]
+            basis[0, i, TOP:high, :] = total + coupling[k] * coupled
+            basis[0, i, low : low + 1, :] = empty
+            basis[0, i, high : high + 1, :] = empty
+        return carry
+
+    lax.fori_loop(0, xs, explicit, 0, unroll=2)
+    zhalo0 = finish_halo(0)
+
+    def explicit_outer(x, zpack):
+        for k in range(species):
+            i = slot(k, x)[0]
+            total = basis[0, i, TOP:high, :] + outer(
+                0, zhalo0, k, x, ahead[1], -back[1], ahead[2], -back[2])
+            basis[0, i, TOP:high, :] = total
             zpack = pack(zpack, total, 1, k, x)
         return zpack
 
-    zsend[1] = lax.fori_loop(0, xs, explicit, jnp.zeros((ys, lanes), jnp.float32), unroll=2)
+    zsend[1] = lax.fori_loop(
+        0, xs, explicit_outer, jnp.zeros((ys, lanes), jnp.float32), unroll=2)
     start_halo(1)
-    zhalo = finish_halo(1)
-
-    def rows0(x, carry):
-        for k in range(species):
-            set_rows(basis, (0,), 1, k, x)
-        return carry
-
-    lax.fori_loop(0, xs, rows0, 0, unroll=4)
 
     cosines, sines, triangle = [], [], []
     target = None
@@ -243,17 +260,28 @@
         return [grid[:, p : p + 1] for p in range(products)]
 
     def implicit(x, carry):
+        for k in range(species):
+            images[0, slot(k, x)[0], TOP:high, :] = applied(basis, (0,), k, x, None)[1]
+        return carry
+
+    lax.fori_loop(0, xs, implicit, 0, unroll=2)
+    zhalo1 = finish_halo(1)
+
+    def implicit_outer(x, carry):
         zpack, cross, square, own = carry
         for k in range(species):
-            here, made = applied(basis, (0,), k, x, zhalo)
-            images[0, slot(k, x)[0], TOP:high, :] = made
+            i = slot(k, x)[0]
+            here = basis[0, i, TOP:high, :]
+            lost = -strength[k]
+            made = images[0, i, TOP:high, :] + outer(1, zhalo1, k, x, lost, lost, lost, lost)
+            images[0, i, TOP:high, :] = made
             zpack = pack(zpack, made, 2, k, x)
             cross = cross + fold(here * made)
             square = square + fold(made * made)
             own = own + fold(here * here)
         return zpack, cross, square, own
 
-    zpack, *parts = lax.fori_loop(0, xs, implicit, (blank, zero, zero, zero), unroll=2)
+    zpack, *parts = lax.fori_loop(0, xs, implicit_outer, (blank, zero, zero, zero), unroll=2)
     share(0, parts)
     zsend[2] = zpack
     start_halo(2)

time: 41 us -> 40.5 us (0.988)
  Pallas kernels: 39.4 us -> 38.9 us
    pallas_call x1, Pallas kernels: 39.4 us -> 38.9 us  [shards(): pl.pallas_call(functools.partial(kernel, ny, nz), out_shape=pltpu.VMEM(st...]
where the time goes in v4:
time: 40.5 us; the launch traced here: 40.3 us
  Pallas kernels  38.9 us (96%)
  local copies, waits for them, and re-layouts  0.8 us (2%)
  between operations  0.66 us (2%)
    pallas_call x1, Pallas kernels, shards(): pl.pallas_call(functools.partial(kernel, ny, nz), out_shape=pltpu.VMEM(st...  38.9 us

profile of v4, /device:TPU:0, one launch (start us, length us, event | category | flops | bytes accessed | tf_op | source)
XLA Modules:
  0.0 40.3 jit_solution(2511916862026425600)
XLA Ops:
  0.7 38.9 %shard_map.64 = f32[1,4,16,16,128]{4,3,2,1,0:T(8,128)S(1)} custom-call(f32[1,4,16,16,128]{4,3,2,1,0:T(8,128)} %state_ref.1, s32[1]{0:T(128)S(6)} %copy.9.set_ref, f32[3,16]{1,0:T(4,128)} %bitcast.5, f32[4,16]{1,0:T(4,128)} %bitcast.6, f32[4,4,16]{2,1,0:T(4,128)} %bitcast.4, f32[4,16]{1,0:T(4,128)} %bitcast.7), custom_call_target="tpu_custom_call" | custom-call | tf_op jit(solution)/shard_map/pallas_call | solution.py:416
  39.5 0.8 %copy.8 = f32[1,4,16,16,128]{4,3,2,1,0:T(8,128)} copy(f32[1,4,16,16,128]{4,3,2,1,0:T(8,128)S(1)} %shard_map.64) | data formatting | bytes 1048576

commit v5 on v4

--- a/solution.py
+++ b/solution.py
@@ -37,9 +37,14 @@
     for table in tables:
         table.start()
 
+    def turns(position, size):
+        return [jnp.where(position + n >= size, position + n - size, position + n)
+                for n in range(size)]
+
+    around_y, around_z = turns(gy, ny), turns(gz, nz)
+
     def peer(step):
-        other = lax.rem(me + step, count)
-        return {"gy": lax.div(other, nz), "gz": lax.rem(other, nz)}
+        return {"gy": around_y[step // nz], "gz": around_z[step % nz]}
 
     barrier = pltpu.get_barrier_semaphore()
     for step in range(1, count):
@@ -222,10 +227,11 @@
         radius = jnp.sqrt(
             entries[column] * entries[column] + entries[column + 1] * entries[column + 1]
         )
-        cosine, sine = entries[column] / radius, entries[column + 1] / radius
+        scale = 1.0 / radius
+        cosine, sine = entries[column] * scale, entries[column + 1] * scale
         cosines.append(cosine)
         sines.append(sine)
-        triangle.append(entries[:column] + [radius])
+        triangle.append(entries[:column] + [scale])
         target.append(-sine * target[column])
         target[column] = cosine * target[column]
 
@@ -381,7 +387,7 @@
         running = target[column]
         for further in range(column + 1, ITERS):
             running = running - triangle[further][column] * coeffs[further]
-        coeffs[column] = running / triangle[column][column]
+        coeffs[column] = running * triangle[column][column]
     coeffs[0] = coeffs[0] * inverse_beta
     wides = [jnp.broadcast_to(c, (ys, lanes)) for c in coeffs]
 

time: 40.5 us -> 40.5 us (level)
  no operation moved by 1% of the time
where the time goes in v5:
time: 40.5 us; the launch traced here: 40.3 us
  Pallas kernels  38.9 us (96%)
  local copies, waits for them, and re-layouts  0.8 us (2%)
  between operations  0.66 us (2%)
    pallas_call x1, Pallas kernels, shards(): pl.pallas_call(functools.partial(kernel, ny, nz), out_shape=pltpu.VMEM(st...  38.9 us

profile of v5, /device:TPU:0, one launch (start us, length us, event | category | flops | bytes accessed | tf_op | source)
XLA Modules:
  0.0 40.3 jit_solution(7444190253816261317)
XLA Ops:
  0.7 38.9 %shard_map.64 = f32[1,4,16,16,128]{4,3,2,1,0:T(8,128)S(1)} custom-call(f32[1,4,16,16,128]{4,3,2,1,0:T(8,128)} %state_ref.1, s32[1]{0:T(128)S(6)} %copy.9.set_ref, f32[3,16]{1,0:T(4,128)} %bitcast.5, f32[4,16]{1,0:T(4,128)} %bitcast.6, f32[4,4,16]{2,1,0:T(4,128)} %bitcast.4, f32[4,16]{1,0:T(4,128)} %bitcast.7), custom_call_target="tpu_custom_call" | custom-call | tf_op jit(solution)/shard_map/pallas_call | solution.py:422
  39.5 0.8 %copy.8 = f32[1,4,16,16,128]{4,3,2,1,0:T(8,128)} copy(f32[1,4,16,16,128]{4,3,2,1,0:T(8,128)S(1)} %shard_map.64) | data formatting | bytes 1048576

commit v6 on v5

--- a/solution.py
+++ b/solution.py
@@ -27,8 +27,14 @@
     low, high = TOP - 1, TOP + ys
     halo_rounds = ITERS + 1
 
-    load = pltpu.make_async_copy(state_ref.at[0], cells, load_sem)
-    load.start()
+    pieces = load_sem.shape[0]
+    width = xs // pieces
+    loads = []
+    for n in range(pieces):
+        part = (slice(None), pl.ds(n * width, width))
+        loads.append(
+            pltpu.make_async_copy(state_ref.at[(0,) + part], cells.at[part], load_sem.at[n]))
+        loads[n].start()
     tables = [
         pltpu.make_async_copy(source, target, table_sem.at[n])
         for n, (source, target) in enumerate((
@@ -147,8 +153,6 @@
             total = total + value[row : row + 8]
         return total
 
-    load.wait()
-
     def take(x, zpack):
         for k in range(species):
             block = cells[k, x]
@@ -159,7 +163,11 @@
             zpack = pack(zpack, block, 0, k, x)
         return zpack
 
-    zsend[0] = lax.fori_loop(0, xs, take, jnp.zeros((ys, lanes), jnp.float32), unroll=2)
+    zpack = jnp.zeros((ys, lanes), jnp.float32)
+    for n in range(pieces):
+        loads[n].wait()
+        zpack = lax.fori_loop(n * width, (n + 1) * width, take, zpack, unroll=2)
+    zsend[0] = zpack
     pl.semaphore_wait(barrier, count - 1)
     start_halo(0)
 
@@ -443,7 +451,7 @@
             pltpu.SemaphoreType.DMA((rounds, 2)),
             pltpu.SemaphoreType.DMA((ITERS,)),
             pltpu.SemaphoreType.DMA((ITERS,)),
-            pltpu.SemaphoreType.DMA,
+            pltpu.SemaphoreType.DMA((4 if xs % 8 == 0 else 1,)),
         ],
         compiler_params=pltpu.CompilerParams(collective_id=0, has_side_effects=True),
     )(state, member_set, *tables)

time: 40.5 us -> 40.5 us (level)
  no operation moved by 1% of the time
where the time goes in v6:
time: 40.5 us; the launch traced here: 40.3 us
  Pallas kernels  38.9 us (96%)
  local copies, waits for them, and re-layouts  0.8 us (2%)
  between operations  0.66 us (2%)
    pallas_call x1, Pallas kernels, shards(): pl.pallas_call(functools.partial(kernel, ny, nz), out_shape=pltpu.VMEM(st...  38.9 us

profile of v6, /device:TPU:0, one launch (start us, length us, event | category | flops | bytes accessed | tf_op | source)
XLA Modules:
  0.0 40.3 jit_solution(14572341956199317926)
XLA Ops:
  0.7 38.9 %shard_map.64 = f32[1,4,16,16,128]{4,3,2,1,0:T(8,128)S(1)} custom-call(f32[1,4,16,16,128]{4,3,2,1,0:T(8,128)} %state_ref.1, s32[1]{0:T(128)S(6)} %copy.9.set_ref, f32[3,16]{1,0:T(4,128)} %bitcast.5, f32[4,16]{1,0:T(4,128)} %bitcast.6, f32[4,4,16]{2,1,0:T(4,128)} %bitcast.4, f32[4,16]{1,0:T(4,128)} %bitcast.7), custom_call_target="tpu_custom_call" | custom-call | tf_op jit(solution)/shard_map/pallas_call | solution.py:430
  39.5 0.8 %copy.8 = f32[1,4,16,16,128]{4,3,2,1,0:T(8,128)} copy(f32[1,4,16,16,128]{4,3,2,1,0:T(8,128)S(1)} %shard_map.64) | data formatting | bytes 1048576
